TPU v7x, 32 devices: a whole 2x2x4 slice. The times are simulated.
32 devices in a mesh: outer: 4 (over y, x), inner: 8 (over z, core).
Axes of the slice: x: 2, y: 2, z: 4, core: 2. Of those that a mesh axis runs over, the one named last changes fastest.
Arguments:
- queries: bfloat16 [8192, 1024], P(('outer', 'inner')), may hold values from -6 to 6
- keys: bfloat16 [2, 8192, 1024], P(None, ('outer', 'inner')), may hold values from -6 to 6
- values: bfloat16 [2, 8192, 1024], P(None, ('outer', 'inner')), may hold values from -6 to 6
- betas: float32 [2, 8, 8192], P(None, None, ('outer', 'inner')), may hold values from 0 to 2
- log_decay: float32 [8, 8192], P(None, ('outer', 'inner')), may hold values from -1 to 0
- out_gain: float32 [128], replicated, may hold values from 0.5 to 1.5
Outputs:
- mixed: bfloat16 [8192, 1024], P(('outer', 'inner'))
All inputs are finite; a program needn't handle non-finite values.
Results may differ from a plain program's by a relative error of at most 0.0018.
Values sent between devices are 32-bit elements; how exact they have to be, the bound alone decides.
A program may use at most 128 MiB of HBM per device.

v0:
```python
import jax
import jax.numpy as jnp
from jax import lax
from jax.sharding import PartitionSpec as P

BLOCK_LEN = 64
HIGHEST = lax.Precision.HIGHEST


def entering(part, axis, combine, identity):
    place = lax.axis_index(axis)
    gathered = jax.tree.map(lambda a: lax.all_gather(a, axis), part)
    state = jax.tree.map(lambda a, e: jnp.zeros_like(a) + jnp.asarray(e, a.dtype), part, identity)

    def one(hop, state):
        return combine(
            state, jax.tree.map(lambda a: lax.dynamic_index_in_dim(a, hop, 0, False), gathered)
        )

    return lax.fori_loop(0, place, one, state)


def spread(x, axis, root):
    mine = lax.axis_index(axis) == root
    return lax.psum(jnp.where(mine, x, jnp.zeros_like(x)), axis)


def prepare(queries, keys, values, betas, log_decay, span):
    length = queries.shape[0]
    heads = betas.shape[1]
    width_k = queries.shape[1] // heads
    width_v = values.shape[2] // heads
    blocks = length // span
    reflect = 2 * span
    query_b = queries.reshape(blocks, span, heads, width_k).transpose(0, 2, 1, 3)
    query_f = query_b.astype(jnp.float32)
    query_inv = lax.rsqrt(jnp.sum(query_f * query_f, -1) + 1e-06)
    query_n = query_f * query_inv[..., None]
    key_b = (
        keys.reshape(2, blocks, span, heads, width_k)
        .transpose(1, 3, 2, 0, 4)
        .reshape(blocks, heads, reflect, width_k)
    )
    key_f = key_b.astype(jnp.float32)
    key_inv = lax.rsqrt(jnp.sum(key_f * key_f, -1) + 1e-06)
    key_n = key_f * key_inv[..., None]
    value_n = (
        values.astype(jnp.float32).reshape(2, blocks, span, heads, width_v).transpose(1, 3, 2, 0, 4)
    )
    value_n = value_n.reshape(blocks, heads, reflect, width_v)
    beta_r = (
        betas.reshape(2, heads, blocks, span).transpose(2, 1, 3, 0).reshape(blocks, heads, reflect)
    )
    decay_t = log_decay.reshape(heads, blocks, span).transpose(1, 0, 2)
    decay_r = jnp.stack([decay_t, jnp.zeros_like(decay_t)], -1).reshape(blocks, heads, reflect)
    cumulative = jnp.cumsum(decay_r, -1)
    row_idx = lax.broadcasted_iota(jnp.int32, (reflect, reflect), 0)
    col_idx = lax.broadcasted_iota(jnp.int32, (reflect, reflect), 1)
    key_gram = (
        jnp.einsum("nhrd,nhsd->nhrs", key_b, key_b, preferred_element_type=jnp.float32)
        * key_inv[..., :, None]
        * key_inv[..., None, :]
    )
    fall_off = jnp.exp(jnp.minimum(cumulative[..., :, None] - cumulative[..., None, :], 0.0))
    strict_low = jnp.where(row_idx > col_idx, key_gram * fall_off, 0.0)
    system = jnp.eye(reflect, dtype=jnp.float32) + beta_r[..., :, None] * strict_low
    scaled = jnp.exp(cumulative)
    right_side = jnp.concatenate(
        [(beta_r * scaled)[..., None] * key_n, beta_r[..., None] * value_n], -1
    )
    solved = lax.linalg.triangular_solve(
        system, right_side, left_side=True, lower=True, unit_diagonal=True
    )
    write_key = solved[..., :width_k]
    write_val = solved[..., width_k:]
    tok_idx = lax.broadcasted_iota(jnp.int32, (span, reflect), 0)
    ref_idx = lax.broadcasted_iota(jnp.int32, (span, reflect), 1)
    query_cum = cumulative.reshape(blocks, heads, span, 2)[..., 1]
    query_key = (
        jnp.einsum("nhcd,nhsd->nhcs", query_b, key_b, preferred_element_type=jnp.float32)
        * query_inv[..., :, None]
        * key_inv[..., None, :]
    )
    fade = jnp.exp(jnp.minimum(query_cum[..., :, None] - cumulative[..., None, :], 0.0))
    reach = jnp.where(ref_idx <= 2 * tok_idx + 1, query_key * fade, 0.0)
    reduced = jnp.exp(query_cum)[..., None] * query_n - jnp.einsum(
        "nhcs,nhsd->nhcd", reach, write_key, precision=HIGHEST
    )
    local_out = jnp.einsum("nhcs,nhsd->nhcd", reach, write_val, precision=HIGHEST)
    last_cum = cumulative[..., -1:]
    tail = jnp.exp(last_cum - cumulative)
    trans = jnp.exp(last_cum)[..., None] * jnp.eye(width_k, dtype=jnp.float32)
    trans = trans - jnp.einsum(
        "nhsd,nhse->nhde", tail[..., None] * write_key, key_n, precision=HIGHEST
    )
    inject = jnp.einsum("nhsd,nhse->nhde", tail[..., None] * write_val, key_n, precision=HIGHEST)
    return (reduced, local_out, trans, inject)


def compose(earlier, later):
    new_map = jnp.einsum("hde,hef->hdf", earlier[0], later[0], precision=HIGHEST)
    new_add = jnp.einsum("hde,hef->hdf", earlier[1], later[0], precision=HIGHEST) + later[1]
    return (new_map, new_add)


def advance(state_pair, inputs):
    prefix_map, prefix_add = state_pair
    red_b, loc_b, trans_b, inj_b = inputs
    carried = jnp.einsum("hcd,hed->hce", red_b, prefix_map, precision=HIGHEST)
    base_out = jnp.einsum("hcd,hed->hce", red_b, prefix_add, precision=HIGHEST) + loc_b
    next_pair = compose((prefix_map, prefix_add), (trans_b, inj_b))
    return (next_pair, (carried, base_out))


def per_device(queries, keys, values, betas, log_decay, out_gain):
    heads = betas.shape[1]
    width_k = queries.shape[1] // heads
    width_v = values.shape[2] // heads
    reduced, local_out, trans, inject = prepare(queries, keys, values, betas, log_decay, BLOCK_LEN)
    identity = (
        jnp.broadcast_to(jnp.eye(width_k, dtype=jnp.float32), (heads, width_k, width_k)),
        jnp.zeros((heads, width_v, width_k), jnp.float32),
    )
    own_pair, pieces = lax.scan(advance, identity, (reduced, local_out, trans, inject))
    carried, base_out = pieces
    before_map, before_add = entering(own_pair, "inner", compose, identity)
    through = compose((before_map, before_add), own_pair)
    group_map, group_add = (
        spread(through[0], "inner", lax.axis_size("inner") - 1),
        spread(through[1], "inner", lax.axis_size("inner") - 1),
    )
    group_state = entering((group_map, group_add), "outer", compose, identity)[1]
    entering_state = (
        jnp.einsum("hde,hef->hdf", group_state, before_map, precision=HIGHEST) + before_add
    )
    readout = jnp.einsum("nhcd,hed->nhce", carried, entering_state, precision=HIGHEST) + base_out
    mean_sq = jnp.mean(readout * readout, -1, keepdims=True)
    normed = readout * lax.rsqrt(mean_sq + 1e-05) * out_gain
    blocks = normed.shape[0]
    return (
        normed.transpose(0, 2, 1, 3)
        .reshape(blocks * BLOCK_LEN, heads * width_v)
        .astype(jnp.bfloat16)
    )


def solution(mesh):
    placed = (
        P(("outer", "inner"), None),
        P(None, ("outer", "inner"), None),
        P(None, ("outer", "inner"), None),
        P(None, None, ("outer", "inner")),
        P(None, ("outer", "inner")),
        P(),
    )
    return jax.shard_map(
        per_device,
        mesh=mesh,
        in_specs=placed,
        out_specs=P(("outer", "inner"), None),
        check_vma=False,
    )
```

profile of v0, /device:TPU:6, one launch (start us, length us, event | category | flops | bytes accessed | tf_op | source)
XLA Modules:
  0.0 689.7 jit_solution(12705137376245005066)
XLA Ops:
  6.5 1.5 copy.206
  8.0 2.3 multiply_reduce_fusion
  10.3 1.1 copy.136
  11.8 1.1 reduce_window_sum.11
  14.4 3.4 add_bitcast_fusion
  17.8 315.9 %custom-call.3 = f32[4,8,1,128,128]{3,4,2,1,0:T(8,128)} custom-call(f32[4,8,1,128,128]{4,3,2,1,0:T(8,128)} %add_bitcast_fusion), custom_call_target="InvertDiagBlocksLowerTriangular" | custom-call | tf_op jit(solution)/shard_map/triangular_solve | solution.py:71
  333.8 2.2 fusion.44
  336.3 1.6 copy.142
  337.9 1.9 broadcast_multiply_fusion
  340.8 6.6 fusion.35
  348.3 3.0 fusion.45
  351.2 3.0 fusion.53
  354.3 6.0 fusion.40
  360.3 6.2 multiply_subtract_fusion
  366.6 31.3 %while.43 = (s32[]{:T(128)}, f32[8,128,128]{1,2,0:T(8,128)S(1)}, f32[8,128,128]{1,2,0:T(8,128)S(1)}, f32[4,8,64,128]{3,2,0,1:T(8,128)}, f32[4,8,64,128]{3,2,0,1:...) while((s32[]{:T(128)}, f32[8,128,128]{1,2,0:T(8,128)S(1)}, ...), condition=%wide.region_4.5_spmd.clone, body=%wide.region_3.4_spmd.clone.sunk | while | flops 604438528 | bytes 8129660 | solution.py:124
  366.6 2.3 fusion.131
  369.0 2.1 fusion.129
  371.1 2.3 fusion.130
  373.4 1.0 convolution_bitcast_fusion.10
  374.5 2.3 fusion.131
  376.8 2.1 fusion.129
  378.9 2.3 fusion.130
  381.2 1.0 convolution_bitcast_fusion.10
  382.3 2.3 fusion.131
  384.6 2.1 fusion.129
  386.7 2.3 fusion.130
  389.0 1.0 convolution_bitcast_fusion.10
  390.1 2.3 fusion.131
  392.4 2.1 fusion.129
  394.5 2.3 fusion.130
  396.8 1.0 convolution_bitcast_fusion.10
  400.0 47.1 %all-gather.11.cloned.1.call-done = f32[64,128,128]{2,1,0:T(8,128)} async-done(((f32[8,128,128]{2,1,0:T(8,128)}), f32[64,128,128]{2,1,0:T(8,128)}) %all-gather.11.cloned.1.call-update) | async-done | bytes 4194320 | tf_op jit(solution)/shard_map/all_gather | solution.py:12
  447.1 47.3 %all-gather.13.cloned.1.call-done = f32[64,128,128]{2,1,0:T(8,128)} async-done(((f32[8,128,128]{2,1,0:T(8,128)}), f32[64,128,128]{2,1,0:T(8,128)}) %all-gather.13.cloned.1.call-update) | async-done | bytes 4194320 | tf_op jit(solution)/shard_map/all_gather | solution.py:12
  494.5 1.0 copy-done.1
  495.5 1.9 fusion.63
  497.4 1.8 fusion.60
  499.3 96.0 %all-reduce.4.cloned.1.call-done = (f32[1,8,128,128]{3,2,1,0:T(8,128)}, f32[1,8,128,128]{3,2,1,0:T(8,128)}) async-done(((f32[1,8,128,128]{3,2,1,0:T(8,128)}, f32[1,8,128,128]{3,2,1,0:T(8,128)}), (f32[1,8,128,128]{3,2,1,0:T(8,128)}, f32[1,8,128,128]{3,2,1,0:T(8,128)})) %all-reduce.4.cloned.1.call-update) | async-done | bytes 1048592 | tf_op jit(solution)/shard_map/psum | solution.py:25
  596.0 34.3 %all-gather.7.cloned.1.call-done = f32[4,8,128,128]{3,2,1,0:T(8,128)} async-done(((f32[1,8,128,128]{3,2,1,0:T(8,128)}), f32[4,8,128,128]{3,2,1,0:T(8,128)}) %all-gather.7.cloned.1.call-update) | async-done | bytes 2097168 | tf_op jit(solution)/shard_map/all_gather | solution.py:12
  630.4 36.9 %all-gather.9.cloned.1.call-done = f32[4,8,128,128]{3,2,1,0:T(8,128)} async-done(((f32[1,8,128,128]{3,2,1,0:T(8,128)}), f32[4,8,128,128]{3,2,1,0:T(8,128)}) %all-gather.9.cloned.1.call-update) | async-done | bytes 2097168 | tf_op jit(solution)/shard_map/all_gather | solution.py:12
  667.3 10.5 %while.42 = (s32[]{:T(128)}, f32[8,128,128]{1,2,0:T(8,128)S(1)}, s32[]{:T(128)}, f32[4,8,128,128]{3,2,1,0:T(8,128)}, f32[4,8,128,128]{3,2,1,0:T(8,128)}, /*index=5*/s32[]{:T(128)}, s32[]{:T(128)}, s32[]{:T(128)}) while((s32[]{:T(128)}, f32[8,128,128]{1,2,0:T(8,128)S(1)}, s32[]{:T(128)}, f32[4,8,128,128]{3,2,1,0:T(8,128)}, ...), condition=%wide.region_10.11_spmd, body=%wide.region_9.10_spmd.sunk | while | flops 201457664 | bytes 5243007 | solution.py:20
  667.3 1.1 constant_dynamic-slice_fusion.5
  668.7 2.1 fusion.120
  670.8 1.1 constant_dynamic-slice_fusion.5
  672.1 2.1 fusion.120
  674.2 1.1 constant_dynamic-slice_fusion.5
  675.5 2.1 fusion.120
  677.9 1.0 fusion.61
  679.1 2.5 multiply_reduce_fusion.1
  (80 shorter events, 9.7 us)
Async XLA Ops:
  6.5 440.6 %all-gather.11.cloned.1.call-start = ((), (), s32[]{:S(2)}) async-start(), calls=%async_computation.2 | async-start | bytes 4718592 | tf_op jit(solution)/shard_map/all_gather | solution.py:12
  8.0 3.4 copy-start.6
  10.3 3.6 copy-start.5
  11.4 342.8 %copy-start = (bf16[2,4,64,8,128]{4,0,2,3,1:T(2,128)(2,1)}, bf16[2,4,64,8,128]{4,0,2,3,1:T(2,128)(2,1)S(1)}, u32[]{:S(2)}) copy-start(bf16[2,4,64,8,128]{4,0,2,3,1:T(2,128)(2,1)S(1)} %copy.136) | copy-start | bytes 3145732
  17.8 318.2 %copy-start.2 = (bf16[2,256,1024]{2,1,0:T(8,128)(2,1)S(1)}, bf16[2,256,1024]{2,1,0:T(8,128)(2,1)}, u32[]{:S(2)}) copy-start(bf16[2,256,1024]{2,1,0:T(8,128)(2,1)} %param.14) | copy-start | bytes 3145732
  337.9 2.2 copy-start.4
  398.9 95.5 %all-gather.13.cloned.1.call-start = ((), (), s32[]{:S(2)}) async-start(), calls=%async_computation.3 | async-start | bytes 4718592 | tf_op jit(solution)/shard_map/all_gather | solution.py:12
  400.0 195.2 %all-reduce.4.cloned.1.call-start = ((), (), s32[]{:S(2)}) async-start(), calls=%async_computation.4 | async-start | bytes 2097152 | tf_op jit(solution)/shard_map/psum | solution.py:25
  494.5 1.0 copy-start.1
  499.2 131.1 %all-gather.7.cloned.1.call-start = ((), (), s32[]{:S(2)}) async-start(), calls=%async_computation | async-start | bytes 2621440 | tf_op jit(solution)/shard_map/all_gather | solution.py:12
  595.3 72.0 %all-gather.9.cloned.1.call-start = ((), (), s32[]{:S(2)}) async-start(), calls=%async_computation.1 | async-start | bytes 2621440 | tf_op jit(solution)/shard_map/all_gather | solution.py:12
  677.9 1.2 copy-start.3
  678.9 2.7 copy-start.7
Sparse Core Ops, SparseCore 0:
  399.0 48.0 all-gather.10
  448.7 45.6 all-gather.12
  499.3 95.8 all-reduce.3
  596.9 33.3 all-gather.6
  632.1 35.1 all-gather.8
where the time goes:
time: 692 us; the launch traced here: 690 us
  other arithmetic  324 us (47%)
  waiting for transfers between devices  262 us (38%)
  matrix products  73.3 us (11%)
  local copies, waits for them, and re-layouts  15.5 us (2%)
  between operations  13.5 us (2%)
    another operation x2, other arithmetic, prepare(): lax.linalg.triangular_solve(system, right_side, left_side=True, lower=Tru...  316 us
    all_gather x4, waiting for transfers between devices, entering(): gathered = jax.tree.map(lambda a: lax.all_gather(a, axis), part)  166 us
    psum x1, waiting for transfers between devices, spread(): return lax.psum(jnp.where(mine, x, jnp.zeros_like(x)), axis)  96 us
    dot_general x8, matrix products, compose(): jnp.einsum('hde,hef->hdf', earlier[1], later[0], precision=HIGHEST)  16.2 us
  transfers between devices with their start and end apart: 5, of which 5 were waited for; matrix products, arithmetic and copies ran while one was open for 0% of the time, Pallas kernels for 0%

commit v1 on v0

--- a/solution.py
+++ b/solution.py
@@ -22,7 +22,7 @@
 
 def spread(x, axis, root):
     mine = lax.axis_index(axis) == root
-    return lax.psum(jnp.where(mine, x, jnp.zeros_like(x)), axis)
+    return jnp.sum(lax.all_gather(jnp.where(mine, x, jnp.zeros_like(x)), axis), axis=0)
 
 
 def prepare(queries, keys, values, betas, log_decay, span):

time: 692 us -> 740 us (1.069)
  waiting for transfers between devices: 262 us -> 288 us
  matrix products: 73.3 us -> 82.6 us
    all_gather x0 -> x2, waiting for transfers between devices: none -> 125 us  [spread(): lax.all_gather(jnp.where(mine, x, jnp.zeros_like(x)), axis)]
    psum x1 -> x0, waiting for transfers between devices: 96 us -> none  [spread(): return lax.psum(jnp.where(mine, x, jnp.zeros_like(x)), axis)]
    dot_general x1, matrix products: 6.01 us -> 15.3 us  [prepare(): jnp.einsum('nhsd,nhse->nhde', tail[..., None] * write_val, key_n, precisi...]
  transfers between devices with their start and end apart: 5 -> 6, of which waited for: 5 -> 6; matrix products, arithmetic and copies ran while one was open for 0% -> 1% of each run, Pallas kernels for 0% -> 0%
where the time goes in v1:
time: 740 us; the launch traced here: 732 us
  other arithmetic  331 us (45%)
  waiting for transfers between devices  288 us (39%)
  matrix products  82.6 us (11%)
  local copies, waits for them, and re-layouts  15.5 us (2%)
  between operations  14.1 us (2%)
    another operation x2, other arithmetic, prepare(): lax.linalg.triangular_solve(system, right_side, left_side=True, lower=Tru...  316 us
    all_gather x4, waiting for transfers between devices, entering(): gathered = jax.tree.map(lambda a: lax.all_gather(a, axis), part)  163 us
    all_gather x2, waiting for transfers between devices, spread(): lax.all_gather(jnp.where(mine, x, jnp.zeros_like(x)), axis)  125 us
    dot_general x8, matrix products, compose(): jnp.einsum('hde,hef->hdf', earlier[1], later[0], precision=HIGHEST)  16.2 us
    dot_general x1, matrix products, prepare(): jnp.einsum('nhsd,nhse->nhde', tail[..., None] * write_val, key_n, precisi...  15.3 us
  transfers between devices with their start and end apart: 6, of which 6 were waited for; matrix products, arithmetic and copies ran while one was open for 1% of the time, Pallas kernels for 0%

profile of v1, /device:TPU:6, one launch (start us, length us, event | category | flops | bytes accessed | tf_op | source)
XLA Modules:
  0.0 732.4 jit_solution(3634140454091514065)
XLA Ops:
  6.5 1.5 copy.204
  8.0 2.3 multiply_reduce_fusion
  10.3 1.1 copy.132
  11.8 1.1 reduce_window_sum.11
  14.4 3.4 add_bitcast_fusion
  17.8 315.9 %custom-call.3 = f32[4,8,1,128,128]{3,4,2,1,0:T(8,128)} custom-call(f32[4,8,1,128,128]{4,3,2,1,0:T(8,128)} %add_bitcast_fusion), custom_call_target="InvertDiagBlocksLowerTriangular" | custom-call | tf_op jit(solution)/shard_map/triangular_solve | solution.py:71
  333.8 2.6 fusion.44
  336.7 1.6 copy.138
  338.3 1.9 broadcast_multiply_fusion
  341.2 6.6 fusion.35
  348.6 3.0 fusion.45
  351.6 3.1 fusion.53
  354.7 15.3 %fusion.40 = f32[4,8,128,128]{2,3,1,0:T(8,128)} fusion(bf16[4,8,128,128]{3,2,1,0:T(8,128)(2,1)S(1)} %bitcast.191, f32[4,8,128,256]{3,2,1,0:T(8,128)S(1)} %fusion.35, f32[4,8,128]{2,1,0:T(8,128)S(1)} %copy.135, f32[4,8,128]{2,1,0:T(8,128)S(1)} %get-tuple-element.294), kind=kOutput, calls=%fused_computation.49 | convolution fusion | flops 806879232 | bytes 5275648 | tf_op jit(solution)/shard_map/nhsd,nhse->nhde/dot_general | solution.py:96
  370.0 6.2 multiply_subtract_fusion
  376.3 31.3 %while.43 = (s32[]{:T(128)}, f32[8,128,128]{1,2,0:T(8,128)S(1)}, f32[8,128,128]{1,2,0:T(8,128)S(1)}, f32[4,8,64,128]{3,2,0,1:T(8,128)}, f32[4,8,64,128]{3,2,0,1:...) while((s32[]{:T(128)}, f32[8,128,128]{1,2,0:T(8,128)S(1)}, ...), condition=%wide.region_4.5_spmd.clone, body=%wide.region_3.4_spmd.clone.sunk | while | flops 604438528 | bytes 8129660 | solution.py:124
  376.3 2.3 fusion.129
  378.6 2.1 fusion.127
  380.7 2.3 fusion.128
  383.0 1.0 convolution_bitcast_fusion.10
  384.2 2.3 fusion.129
  386.5 2.1 fusion.127
  388.6 2.3 fusion.128
  390.9 1.0 convolution_bitcast_fusion.10
  392.0 2.3 fusion.129
  394.3 2.1 fusion.127
  396.4 2.3 fusion.128
  398.7 1.0 convolution_bitcast_fusion.10
  399.8 2.3 fusion.129
  402.1 2.1 fusion.127
  404.2 2.3 fusion.128
  409.7 47.1 %all-gather.13.cloned.1.call-done = f32[64,128,128]{2,1,0:T(8,128)} async-done(((f32[8,128,128]{2,1,0:T(8,128)}), f32[64,128,128]{2,1,0:T(8,128)}) %all-gather.13.cloned.1.call-update) | async-done | bytes 4194320 | tf_op jit(solution)/shard_map/all_gather | solution.py:12
  456.8 47.3 %all-gather.15.cloned.1.call-done = f32[64,128,128]{2,1,0:T(8,128)} async-done(((f32[8,128,128]{2,1,0:T(8,128)}), f32[64,128,128]{2,1,0:T(8,128)}) %all-gather.15.cloned.1.call-update) | async-done | bytes 4194320 | tf_op jit(solution)/shard_map/all_gather | solution.py:12
  505.2 1.8 fusion.61
  507.1 1.8 convolution_select_fusion
  509.0 81.6 %all-gather.21.cloned.1.call-done = f32[64,128,128]{2,1,0:T(8,128)} async-done(((f32[8,128,128]{2,1,0:T(8,128)}), f32[64,128,128]{2,1,0:T(8,128)}) %all-gather.21.cloned.1.call-update) | async-done | bytes 4194320 | tf_op jit(solution)/shard_map/all_gather | solution.py:25
  590.6 3.3 reduce_sum.48
  594.0 43.8 %all-gather.17.cloned.1.call-done = f32[64,128,128]{2,1,0:T(8,128)} async-done(((f32[8,128,128]{2,1,0:T(8,128)}), f32[64,128,128]{2,1,0:T(8,128)}) %all-gather.17.cloned.1.call-update) | async-done | bytes 4194320 | tf_op jit(solution)/shard_map/all_gather | solution.py:25
  637.8 3.3 reduce_sum.47
  641.3 31.3 %all-gather.23.cloned.1.call-done = f32[32,128,128]{2,1,0:T(8,128)} async-done(((f32[8,128,128]{2,1,0:T(8,128)}), f32[32,128,128]{2,1,0:T(8,128)}) %all-gather.23.cloned.1.call-update) | async-done | bytes 2097168 | tf_op jit(solution)/shard_map/all_gather | solution.py:12
  672.6 36.9 %all-gather.19.cloned.1.call-done = f32[32,128,128]{2,1,0:T(8,128)} async-done(((f32[8,128,128]{2,1,0:T(8,128)}), f32[32,128,128]{2,1,0:T(8,128)}) %all-gather.19.cloned.1.call-update) | async-done | bytes 2097168 | tf_op jit(solution)/shard_map/all_gather | solution.py:12
  709.5 10.5 %while.42 = (s32[]{:T(128)}, f32[8,128,128]{1,2,0:T(8,128)S(1)}, s32[]{:T(128)}, f32[4,8,128,128]{3,2,1,0:T(8,128)}, f32[4,8,128,128]{3,2,1,0:T(8,128)}, /*index=5*/s32[]{:T(128)}, s32[]{:T(128)}, s32[]{:T(128)}) while((s32[]{:T(128)}, f32[8,128,128]{1,2,0:T(8,128)S(1)}, s32[]{:T(128)}, f32[4,8,128,128]{3,2,1,0:T(8,128)}, ...), condition=%wide.region_10.11_spmd, body=%wide.region_9.10_spmd.sunk | while | flops 201457664 | bytes 5243007 | solution.py:20
  709.5 1.1 constant_dynamic-slice_fusion.5
  710.9 2.1 fusion.118
  713.0 1.1 constant_dynamic-slice_fusion.5
  714.3 2.1 fusion.118
  716.4 1.1 constant_dynamic-slice_fusion.5
  717.7 2.1 fusion.118
  721.2 2.5 multiply_reduce_fusion.1
  (85 shorter events, 12.3 us)
Async XLA Ops:
  6.5 450.3 %all-gather.13.cloned.1.call-start = ((), (), s32[]{:S(2)}) async-start(), calls=%async_computation | async-start | bytes 4718592 | tf_op jit(solution)/shard_map/all_gather | solution.py:12
  8.0 3.4 copy-start.6
  10.3 3.6 copy-start.5
  11.4 343.3 %copy-start = (bf16[2,4,64,8,128]{4,0,2,3,1:T(2,128)(2,1)}, bf16[2,4,64,8,128]{4,0,2,3,1:T(2,128)(2,1)S(1)}, u32[]{:S(2)}) copy-start(bf16[2,4,64,8,128]{4,0,2,3,1:T(2,128)(2,1)S(1)} %copy.132) | copy-start | bytes 3145732
  17.8 318.6 %copy-start.2 = (bf16[2,256,1024]{2,1,0:T(8,128)(2,1)S(1)}, bf16[2,256,1024]{2,1,0:T(8,128)(2,1)}, u32[]{:S(2)}) copy-start(bf16[2,256,1024]{2,1,0:T(8,128)(2,1)} %param.14) | copy-start | bytes 3145732
  338.3 2.2 copy-start.4
  408.6 95.5 %all-gather.15.cloned.1.call-start = ((), (), s32[]{:S(2)}) async-start(), calls=%async_computation.1 | async-start | bytes 4718592 | tf_op jit(solution)/shard_map/all_gather | solution.py:12
  409.7 180.9 %all-gather.21.cloned.1.call-start = ((), (), s32[]{:S(2)}) async-start(), calls=%async_computation.4 | async-start | bytes 4718592 | tf_op jit(solution)/shard_map/all_gather | solution.py:25
  504.2 1.0 copy-start.1
  507.1 130.7 %all-gather.17.cloned.1.call-start = ((), (), s32[]{:S(2)}) async-start(), calls=%async_computation.2 | async-start | bytes 4718592 | tf_op jit(solution)/shard_map/all_gather | solution.py:25
  508.9 163.6 %all-gather.23.cloned.1.call-start = ((), (), s32[]{:S(2)}) async-start(), calls=%async_computation.5 | async-start | bytes 2621440 | tf_op jit(solution)/shard_map/all_gather | solution.py:12
  593.9 115.5 %all-gather.19.cloned.1.call-start = ((), (), s32[]{:S(2)}) async-start(), calls=%async_computation.3 | async-start | bytes 2621440 | tf_op jit(solution)/shard_map/all_gather | solution.py:12
  720.0 1.2 copy-start.3
  721.0 2.7 copy-start.7
Sparse Core Ops, SparseCore 0:
  408.7 48.0 all-gather.12
  458.4 45.6 all-gather.14
  507.2 83.3 all-gather.20
  592.1 45.6 all-gather.16
  639.5 33.0 all-gather.22
  674.3 35.1 all-gather.18
